TPU v7x, 32 devices: a whole 2x2x4 slice. The times are simulated.
32 devices in a mesh: grp: 4 (over x, core), dev: 8 (over z, y).
Axes of the slice: x: 2, y: 2, z: 4, core: 2. Of those that a mesh axis runs over, the one named last changes fastest.
Arguments:
- features: bfloat16 [24576, 512], P(('grp', 'dev')), may hold values from -6 to 6
- grad_out: bfloat16 [24576, 512], P(('grp', 'dev')), may hold values from -6 to 6
- w_self: bfloat16 [512, 512], replicated, may hold values from -0.25 to 0.25
- w_neigh: bfloat16 [512, 512], replicated, may hold values from -0.25 to 0.25
- neighbours: int32 [24576, 32], P(('grp', 'dev')), may hold values from 0 to 895, as said below
- degree: int32 [24576], P(('grp', 'dev')), may hold values from 8 to 32
- send_rows: int32 [256, 8], P(('grp', 'dev')), may hold values from 0 to 767
- hub_rows: int32 [64], P(('grp', 'dev')), may hold values from 0 to 767, as said below
Outputs:
- output: bfloat16 [24576, 512], P(('grp', 'dev'))
- grad_features: bfloat16 [24576, 512], P(('grp', 'dev'))
Inputs may be any that keep to these rules, and one draw needn't show every extreme that they name: `neighbours`: codes below 768 name rows of the node's device, the next 64 name rows listed for it by its group, the last 64 name hub nodes. Slot 0 of every node holds a listed row and slot 1 a hub; every listed row of a device is named by some node of the reading device and every hub by some node. `hub_rows`: the 2 entries of one device are distinct rows of that device.
All inputs are finite; a program needn't handle non-finite values.
Results may differ from a plain program's by a relative error of at most 0.0051.
Values may be sent and summed in bfloat16 or wider, within the bound.
A program may use at most 64 MiB of HBM per device.

v0:
```python
import math
import jax
import jax.numpy as jnp
from jax import lax
from jax.sharding import PartitionSpec as P


def count_tiles(slot_codes, keep_mask, tile_width, first_code):
    column_ids = first_code + lax.iota(jnp.int32, tile_width)
    matches = (slot_codes[:, :, None] == column_ids[None, None, :]) & keep_mask[:, :, None]
    return jnp.sum(matches.astype(jnp.bfloat16), axis=1)


def local(features, grad_out, w_self, w_neigh, neighbours, degree, send_rows, hub_rows):
    row_count, feat_width = features.shape
    slot_count = neighbours.shape[1]
    groups = lax.axis_size("grp")
    members = lax.axis_size("dev")
    halo_count = send_rows.shape[0] * send_rows.shape[1]
    owned_hubs = hub_rows.shape[0]
    hub_count = owned_hubs * groups * members
    keep_slots = lax.iota(jnp.int32, slot_count)[None, :] < degree[:, None]
    block_rows = math.gcd(row_count, 256)
    block_total = row_count // block_rows

    def build_tiles(block_args):
        slot_codes, keep_mask = block_args
        return (
            count_tiles(slot_codes, keep_mask, row_count, 0),
            count_tiles(slot_codes, keep_mask, halo_count, row_count),
            count_tiles(slot_codes, keep_mask, hub_count, row_count + halo_count),
        )

    tile_local, tile_halo, tile_hub = lax.map(
        build_tiles,
        (
            neighbours.reshape(block_total, block_rows, slot_count),
            keep_slots.reshape(block_total, block_rows, slot_count),
        ),
    )
    tile_local = tile_local.reshape(row_count, row_count)
    tile_halo = tile_halo.reshape(row_count, halo_count)
    tile_hub = tile_hub.reshape(row_count, hub_count)
    send_list = send_rows.reshape(halo_count)
    outgoing = jnp.take(features, send_list, axis=0)
    incoming = lax.all_to_all(outgoing, "dev", split_axis=0, concat_axis=0, tiled=True)
    summed = jnp.dot(tile_local, features, preferred_element_type=jnp.float32)
    summed = summed + jnp.dot(tile_halo, incoming, preferred_element_type=jnp.float32)
    hub_own = jnp.take(features, hub_rows, axis=0)
    tile_cols = tile_hub
    summed = summed + jnp.dot(
        tile_cols,
        lax.all_gather(hub_own, ("grp", "dev"), axis=0, tiled=True),
        preferred_element_type=jnp.float32,
    )
    degree_f = degree.astype(jnp.float32)[:, None]
    neigh_mean = (summed / degree_f).astype(jnp.bfloat16)
    preact = jnp.dot(features, w_self, preferred_element_type=jnp.float32) + jnp.dot(
        neigh_mean, w_neigh, preferred_element_type=jnp.float32
    )
    output = jax.nn.silu(preact).astype(jnp.bfloat16)
    sigmoid_pre = jax.nn.sigmoid(preact)
    gated = (
        grad_out.astype(jnp.float32) * sigmoid_pre * (1.0 + preact * (1.0 - sigmoid_pre))
    ).astype(jnp.bfloat16)
    contract_last = (((1,), (1,)), ((), ()))
    contract_first = (((0,), (0,)), ((), ()))
    grad_self = lax.dot_general(gated, w_self, contract_last, preferred_element_type=jnp.float32)
    scaled = (
        lax.dot_general(gated, w_neigh, contract_last, preferred_element_type=jnp.float32)
        / degree_f
    ).astype(jnp.bfloat16)
    grad_total = grad_self + lax.dot_general(
        tile_local, scaled, contract_first, preferred_element_type=jnp.float32
    )
    halo_partial = lax.dot_general(
        tile_halo, scaled, contract_first, preferred_element_type=jnp.float32
    )
    returned = lax.all_to_all(
        halo_partial.astype(jnp.bfloat16), "dev", split_axis=0, concat_axis=0, tiled=True
    ).astype(halo_partial.dtype)
    grad_total = grad_total + jax.ops.segment_sum(returned, send_list, num_segments=row_count)
    tile_cols = tile_hub
    mine = lax.psum_scatter(
        lax.dot_general(tile_cols, scaled, contract_first, preferred_element_type=jnp.float32),
        ("grp", "dev"),
        scatter_dimension=0,
        tiled=True,
    )
    grad_total = grad_total + jax.ops.segment_sum(mine, hub_rows, num_segments=row_count)
    return (output, grad_total.astype(jnp.bfloat16))


def solution(mesh):
    placed = (
        P(("grp", "dev"), None),
        P(("grp", "dev"), None),
        P(),
        P(),
        P(("grp", "dev"), None),
        P(("grp", "dev")),
        P(("grp", "dev"), None),
        P(("grp", "dev")),
    )
    return jax.shard_map(
        local,
        mesh=mesh,
        in_specs=placed,
        out_specs=(P(("grp", "dev"), None), P(("grp", "dev"), None)),
        check_vma=False,
    )
```

profile of v0, /device:TPU:0, one launch (start us, length us, event | category | flops | bytes accessed | tf_op | source)
XLA Modules:
  0.0 273.5 jit_solution(13714239355453946839)
XLA Ops:
  7.2 0.8 reshape.95
  10.1 7.3 %all-to-all-start = ((bf16[8,8,512]{2,1,0:T(8,128)(2,1)}), bf16[8,8,512]{2,1,0:T(8,128)(2,1)S(1)}, u32[]{:S(2)}, u32[]{:S(2)}) async-start(bf16[8,8,512]{2,1,0:T(8,128)(2,1)} %bitcast_select_fusion), calls=%async_computation | async-start | bytes 131072 | tf_op jit(solution)/shard_map/all_to_all | solution.py:46
  18.8 0.9 reshape.92
  20.5 23.6 %while.17 = (s32[]{:T(128)}, bf16[3,256,768]{2,1,0:T(8,128)(2,1)S(1)}, bf16[3,256,64]{1,2,0:T(8,128)(2,1)S(1)}, bf16[3,256,64]{1,2,0:T(8,128)(2,1)S(1)}, s32[3,2...) while((s32[]{:T(128)}, bf16[3,256,768]{2,1,0:T(8,128)(2,1)S(1)}, ...), condition=%wide.region_4.5_spmd, body=%wide.region_0.4_spmd.sunk | while | flops 29130880 | bytes 1688669 | solution.py:34
  20.6 0.8 fusion.40
  21.6 6.7 %fusion.39 = bf16[256,768]{1,0:T(8,128)(2,1)S(1)} fusion(s32[256,32]{1,0:T(8,128)S(1)} %bitcast.64, pred[256,32]{1,0:T(8,128)(4,1)S(1)} %copy.29), kind=kLoop, calls=%fused_computation.6.clone.1 | loop fusion | flops 24969216 | bytes 434176 | tf_op jit(solution)/shard_map/while/body/eval_jaxpr/reduce_sum | solution.py:11
  28.4 0.8 fusion.40
  29.5 6.7 %fusion.39 = bf16[256,768]{1,0:T(8,128)(2,1)S(1)} fusion(s32[256,32]{1,0:T(8,128)S(1)} %bitcast.64, pred[256,32]{1,0:T(8,128)(4,1)S(1)} %copy.29), kind=kLoop, calls=%fused_computation.6.clone.1 | loop fusion | flops 24969216 | bytes 434176 | tf_op jit(solution)/shard_map/while/body/eval_jaxpr/reduce_sum | solution.py:11
  36.3 0.8 fusion.40
  37.3 6.7 %fusion.39 = bf16[256,768]{1,0:T(8,128)(2,1)S(1)} fusion(s32[256,32]{1,0:T(8,128)S(1)} %bitcast.64, pred[256,32]{1,0:T(8,128)(4,1)S(1)} %copy.29), kind=kLoop, calls=%fused_computation.6.clone.1 | loop fusion | flops 24969216 | bytes 434176 | tf_op jit(solution)/shard_map/while/body/eval_jaxpr/reduce_sum | solution.py:11
  44.1 1.0 copy-done.3
  45.1 1.9 fusion.16
  47.1 1.7 fusion.15
  49.5 68.1 %all-gather = bf16[32,2,512]{2,1,0:T(2,128)(2,1)S(1)} all-gather(bf16[1,2,512]{2,1,0:T(2,128)(2,1)S(1)} %fusion.13), channel_id=1, replica_groups=mesh['grp'=4,'dev'=8] {'grp','dev'}, dimensions={0}, use_global_device_ids=true | all-gather | bytes 67584 | tf_op jit(solution)/shard_map/all_gather | solution.py:53
  118.1 4.9 %multiply_convert_fusion = (bf16[768,512]{1,0:T(8,128)(2,1)}, bf16[768,512]{1,0:T(8,128)(2,1)}) fusion(bf16[768,512]{1,0:T(8,128)(2,1)} %param.11, f32[768,512]{1,0:T(8,128)} %fusion.15, bf16[512,512]{1,0:T(8,128)(2,1)} %param.13, f32[768,512]{1,0:T(8,128)} %fusion.16, f32[768,512]{1,0:T(8,128)S(1)} %fusion.11, bf16[768,64]{0,1:T(8,128)(2,1)S(1)} %bitcast.68, ...), kind=kOutput, calls=%fused_computation.20 | convolution fusion | flops 459669504 | bytes 7769088 | tf_op jit(solution)/shard_map/dot_general | solution.py:58
  123.0 2.0 divide_convert_fusion
  125.0 2.0 fusion.17
  127.0 0.9 fusion.5
  127.9 0.9 fusion.18
  128.8 3.3 %all-to-all-start.1 = ((bf16[8,8,512]{2,1,0:T(8,128)(2,1)}), bf16[8,8,512]{2,1,0:T(8,128)(2,1)S(1)}, u32[]{:S(2)}, u32[]{:S(2)}) async-start(bf16[8,8,512]{2,1,0:T(8,128)(2,1)} %fusion.5), calls=%async_computation.1 | async-start | bytes 131072 | tf_op jit(solution)/shard_map/all_to_all | solution.py:79
  132.9 2.3 convolution_add_fusion
  135.1 128.2 %all-reduce.3.cloned.1.call-done = f32[64,512]{1,0:T(8,128)} async-done(((f32[64,512]{1,0:T(8,128)}), f32[64,512]{1,0:T(8,128)}) %all-reduce.3.cloned.1.call-update) | async-done | bytes 131088
  264.1 1.6 scatter_custom_fusion
  265.7 1.0 convert_element_type.66
  (65 shorter events, 7.8 us)
Async XLA Ops:
  7.2 1.6 copy-start
  10.1 107.6 %all-to-all-start = ((bf16[8,8,512]{2,1,0:T(8,128)(2,1)}), bf16[8,8,512]{2,1,0:T(8,128)(2,1)S(1)}, u32[]{:S(2)}, u32[]{:S(2)}) async-start(bf16[8,8,512]{2,1,0:T(8,128)(2,1)} %bitcast_select_fusion), calls=%async_computation | async-start | bytes 131072 | tf_op jit(solution)/shard_map/all_to_all | solution.py:46
  44.1 1.0 copy-start.3
  45.1 1.9 copy-start.1
  47.1 70.5 %copy-start.2 = (s32[768]{0:T(1024)S(1)}, s32[768]{0:T(1024)}, u32[]{:S(2)}) copy-start(s32[768]{0:T(1024)} %param.15) | copy-start | bytes 9220
  47.1 70.6 %copy-start.5 = (s32[2]{0:T(128)S(1)}, s32[2]{0:T(128)}, u32[]{:S(2)}) copy-start(s32[2]{0:T(128)} %param.17) | copy-start | bytes 28
  123.0 2.0 copy-start.4
  128.8 135.3 %all-to-all-start.1 = ((bf16[8,8,512]{2,1,0:T(8,128)(2,1)}), bf16[8,8,512]{2,1,0:T(8,128)(2,1)S(1)}, u32[]{:S(2)}, u32[]{:S(2)}) async-start(bf16[8,8,512]{2,1,0:T(8,128)(2,1)} %fusion.5), calls=%async_computation.1 | async-start | bytes 131072 | tf_op jit(solution)/shard_map/all_to_all | solution.py:79
  132.1 131.2 %all-reduce.3.cloned.1.call-start = ((), (), s32[]{:S(2)}) async-start(), calls=%async_computation.2 | async-start | bytes 262144
Sparse Core Ops, SparseCore 0:
  138.5 124.8 all-reduce.2
where the time goes:
time: 274 us
  waiting for transfers between devices  129 us (47%)
  blocking collectives  68.1 us (25%)
  other arithmetic  27.9 us (10%)
  matrix products  16.9 us (6%)
  between operations  14.2 us (5%)
  starting transfers between devices  10.7 us (4%)
  local copies, waits for them, and re-layouts  6.51 us (2%)
    unnamed x2, waiting for transfers between devices  129 us
    all_gather x1, blocking collectives, local(): lax.all_gather(hub_own, ('grp', 'dev'), axis=0, tiled=True)  68.1 us
    reduce_sum x6, other arithmetic, count_tiles(): return jnp.sum(matches.astype(jnp.bfloat16), axis=1)  22.4 us
    all_to_all x1, starting transfers between devices, local(): lax.all_to_all(outgoing, 'dev', split_axis=0, concat_axis=0, tiled=True)  7.31 us
  transfers between devices with their start and end apart: 3, of which 1 were waited for; matrix products, arithmetic and copies ran while one was open for 12% of the time, Pallas kernels for 0%

commit v1 on v0

--- a/solution.py
+++ b/solution.py
@@ -48,11 +48,23 @@
     summed = summed + jnp.dot(tile_halo, incoming, preferred_element_type=jnp.float32)
     hub_own = jnp.take(features, hub_rows, axis=0)
     tile_cols = tile_hub
-    summed = summed + jnp.dot(
-        tile_cols,
-        lax.all_gather(hub_own, ("grp", "dev"), axis=0, tiled=True),
-        preferred_element_type=jnp.float32,
-    )
+
+    def _change_modes(here_x):
+        inter = lax.axis_size(("grp", "dev"))
+        current_arr = lax.axis_index(("grp", "dev"))
+        next_value, back, heard = (inter, current_arr, here_x.shape[0])
+        o_now, p_next = (here_x, 1)
+        while p_next < next_value:
+            z2 = range(next_value)
+            block_out = map(lambda u: (u, (u - p_next) % next_value), z2)
+            front = list(block_out)
+            o_now = jnp.concatenate(
+                [o_now, lax.ppermute(o_now, axis_name=("grp", "dev"), perm=front)], 0
+            )
+            p_next = 2 * p_next
+        return jnp.roll(o_now, back * heard, 0)
+
+    summed = summed + jnp.dot(tile_cols, _change_modes(hub_own), preferred_element_type=jnp.float32)
     degree_f = degree.astype(jnp.float32)[:, None]
     neigh_mean = (summed / degree_f).astype(jnp.bfloat16)
     preact = jnp.dot(features, w_self, preferred_element_type=jnp.float32) + jnp.dot(

time: 274 us -> 219 us (0.80)
  blocking collectives: 68.1 us -> 0 us
  starting transfers between devices: 10.7 us -> 17.7 us
  waiting for transfers between devices: 129 us -> 134 us
    all_gather x1 -> x0, blocking collectives: 68.1 us -> none  [local(): lax.all_gather(hub_own, ('grp', 'dev'), axis=0, tiled=True)]
    ppermute x0 -> x5, starting transfers between devices: none -> 11 us  [_change_modes(): lax.ppermute(o_now, axis_name=('grp', 'dev'), perm=front)]
    ppermute x0 -> x5, waiting for transfers between devices: none -> 4.91 us  [_change_modes(): lax.ppermute(o_now, axis_name=('grp', 'dev'), perm=front)]
    all_to_all x1, starting transfers between devices: 7.31 us -> 3.35 us  [local(): lax.all_to_all(outgoing, 'dev', split_axis=0, concat_axis=0, tiled=True)]
  transfers between devices with their start and end apart: 3 -> 8, of which waited for: 1 -> 3; matrix products, arithmetic and copies ran while one was open for 12% -> 16% of each run, Pallas kernels for 0% -> 0%
where the time goes in v1:
time: 219 us
  waiting for transfers between devices  134 us (61%)
  other arithmetic  28 us (13%)
  matrix products  18.1 us (8%)
  starting transfers between devices  17.7 us (8%)
  between operations  14.2 us (6%)
  local copies, waits for them, and re-layouts  6.37 us (3%)
    unnamed x2, waiting for transfers between devices  129 us
    reduce_sum x6, other arithmetic, count_tiles(): return jnp.sum(matches.astype(jnp.bfloat16), axis=1)  22.3 us
    ppermute x5, starting transfers between devices, _change_modes(): lax.ppermute(o_now, axis_name=('grp', 'dev'), perm=front)  11 us
    ppermute x5, waiting for transfers between devices, _change_modes(): lax.ppermute(o_now, axis_name=('grp', 'dev'), perm=front)  4.91 us
    dot_general x1, matrix products, local(): jnp.dot(neigh_mean, w_neigh, preferred_element_type=jnp.float32)  4.86 us
  transfers between devices with their start and end apart: 8, of which 3 were waited for; matrix products, arithmetic and copies ran while one was open for 16% of the time, Pallas kernels for 0%

profile of v1, /device:TPU:0, one launch (start us, length us, event | category | flops | bytes accessed | tf_op | source)
XLA Modules:
  0.0 218.8 jit_solution(13168533487759379695)
XLA Ops:
  9.2 6.4 %collective-permute-start = (bf16[2,512]{1,0:T(2,128)(2,1)S(1)}, bf16[2,512]{1,0:T(2,128)(2,1)S(1)}, u32[]{:S(2)}, u32[]{:S(2)}) collective-permute-start(bf16[2,512]{1,0:T(2,128)(2,1)S(1)} %broadcast_select_fusion), channel_id=1, source_target_pairs={{0,31},{1,0},{2,1},{3,2},{4,3},{5,4},{6,5},{7,6},{8,7},{9,8},{10,9... | collective-permute-start | bytes 6152 | tf_op jit(solution)/shard_map/ppermute | solution.py:62
  15.6 0.8 reshape.95
  18.5 3.4 %all-to-all-start = ((bf16[8,8,512]{2,1,0:T(8,128)(2,1)}), bf16[8,8,512]{2,1,0:T(8,128)(2,1)S(1)}, u32[]{:S(2)}, u32[]{:S(2)}) async-start(bf16[8,8,512]{2,1,0:T(8,128)(2,1)} %bitcast_select_fusion), calls=%async_computation | async-start | bytes 131072 | tf_op jit(solution)/shard_map/all_to_all | solution.py:46
  22.6 0.9 reshape.92
  23.6 3.8 %collective-permute-start.1 = (bf16[4,512]{1,0:T(4,128)(2,1)S(1)}, bf16[4,512]{1,0:T(4,128)(2,1)S(1)}, u32[]{:S(2)}, u32[]{:S(2)}) collective-permute-start(bf16[4,512]{1,0:T(4,128)(2,1)S(1)} %pad_maximum_fusion.2), channel_id=1, source_target_pairs={{0,30},{1,31},{2,0},{3,1},{4,2},{5,3},{6,4},{7,5},{8,6},{9,7},{10,... | collective-permute-start | bytes 12296 | tf_op jit(solution)/shard_map/ppermute | solution.py:62
  27.4 23.5 %while.17 = (s32[]{:T(128)}, bf16[3,256,768]{2,1,0:T(8,128)(2,1)S(1)}, bf16[3,256,64]{1,2,0:T(8,128)(2,1)S(1)}, bf16[3,256,64]{1,2,0:T(8,128)(2,1)S(1)}, s32[3,2...) while((s32[]{:T(128)}, bf16[3,256,768]{2,1,0:T(8,128)(2,1)S(1)}, ...), condition=%wide.region_4.5_spmd, body=%wide.region_0.4_spmd.sunk | while | flops 29130880 | bytes 1688669 | solution.py:34
  28.5 6.7 %fusion.43 = bf16[256,768]{1,0:T(8,128)(2,1)S(1)} fusion(s32[256,32]{1,0:T(8,128)S(1)} %bitcast.61, pred[256,32]{1,0:T(8,128)(4,1)S(1)} %copy.29), kind=kLoop, calls=%fused_computation.6.clone.1 | loop fusion | flops 24969216 | bytes 434176 | tf_op jit(solution)/shard_map/while/body/eval_jaxpr/reduce_sum | solution.py:11
  36.4 6.7 %fusion.43 = bf16[256,768]{1,0:T(8,128)(2,1)S(1)} fusion(s32[256,32]{1,0:T(8,128)S(1)} %bitcast.61, pred[256,32]{1,0:T(8,128)(4,1)S(1)} %copy.29), kind=kLoop, calls=%fused_computation.6.clone.1 | loop fusion | flops 24969216 | bytes 434176 | tf_op jit(solution)/shard_map/while/body/eval_jaxpr/reduce_sum | solution.py:11
  44.2 6.7 %fusion.43 = bf16[256,768]{1,0:T(8,128)(2,1)S(1)} fusion(s32[256,32]{1,0:T(8,128)S(1)} %bitcast.61, pred[256,32]{1,0:T(8,128)(4,1)S(1)} %copy.29), kind=kLoop, calls=%fused_computation.6.clone.1 | loop fusion | flops 24969216 | bytes 434176 | tf_op jit(solution)/shard_map/while/body/eval_jaxpr/reduce_sum | solution.py:11
  51.1 0.9 copy-done.3
  52.0 1.9 fusion.21
  53.9 1.7 collective-permute-done.2
  55.7 1.7 fusion.20
  58.2 3.2 %collective-permute-done.4 = bf16[32,512]{1,0:T(8,128)(2,1)S(1)} collective-permute-done((bf16[32,512]{1,0:T(8,128)(2,1)S(1)}, bf16[32,512]{1,0:T(8,128)(2,1)S(1)}, u32[]{:S(2)}, u32[]{:S(2)}) %collective-permute-start.4) | collective-permute-done | bytes 32800 | tf_op jit(solution)/shard_map/ppermute | solution.py:62
  61.9 4.9 %multiply_convert_fusion = (bf16[768,512]{1,0:T(8,128)(2,1)}, bf16[768,512]{1,0:T(8,128)(2,1)}) fusion(bf16[768,512]{1,0:T(8,128)(2,1)} %param.11, f32[768,512]{1,0:T(8,128)} %fusion.20, bf16[512,512]{1,0:T(8,128)(2,1)} %param.13, f32[768,512]{1,0:T(8,128)} %fusion.21, f32[768,512]{1,0:T(8,128)S(1)} %fusion.11, bf16[768,64]{0,1:T(8,128)(2,1)S(1)} %bitcast.65, ...), kind=kOutput, calls=%fused_computation.20 | convolution fusion | flops 459669504 | bytes 7770116 | tf_op jit(solution)/shard_map/dot_general | solution.py:70
  66.8 1.9 divide_convert_fusion
  68.7 0.9 fusion.5
  69.5 0.9 fusion.23
  70.5 3.2 %fusion.22 = f32[768,512]{1,0:T(8,128)} fusion(bf16[768,768]{1,0:T(8,128)(2,1)} %bitcast.70, bf16[768,512]{1,0:T(8,128)(2,1)S(1)} %divide_convert_fusion), kind=kOutput, calls=%fused_computation.56 | convolution fusion | flops 603979776 | bytes 3538944 | tf_op jit(solution)/shard_map/dot_general | solution.py:85
  73.7 3.3 %all-to-all-start.1 = ((bf16[8,8,512]{2,1,0:T(8,128)(2,1)}), bf16[8,8,512]{2,1,0:T(8,128)(2,1)S(1)}, u32[]{:S(2)}, u32[]{:S(2)}) async-start(bf16[8,8,512]{2,1,0:T(8,128)(2,1)} %fusion.5), calls=%async_computation.1 | async-start | bytes 131072 | tf_op jit(solution)/shard_map/all_to_all | solution.py:91
  77.8 2.3 %convolution_add_fusion = f32[768,512]{1,0:T(8,128)S(1)} fusion(f32[768,512]{1,0:T(8,128)} %fusion.22, bf16[768,512]{1,0:T(8,128)(2,1)} %get-tuple-element.125, bf16[512,512]{1,0:T(8,128)(2,1)S(1)} %copy-done.1), kind=kOutput, calls=%fused_computation.24 | convolution fusion | flops 403046400 | bytes 4456448 | tf_op jit(solution)/shard_map/dot_general | solution.py:80
  80.0 128.6 %all-reduce.3.cloned.1.call-done = f32[64,512]{1,0:T(8,128)} async-done(((f32[64,512]{1,0:T(8,128)}), f32[64,512]{1,0:T(8,128)}) %all-reduce.3.cloned.1.call-update) | async-done | bytes 131088
  209.4 1.6 scatter_custom_fusion
  211.0 1.0 convert_element_type.66
  (76 shorter events, 11.0 us)
Async XLA Ops:
  7.2 1.4 copy-start
  9.2 14.3 %collective-permute-start = (bf16[2,512]{1,0:T(2,128)(2,1)S(1)}, bf16[2,512]{1,0:T(2,128)(2,1)S(1)}, u32[]{:S(2)}, u32[]{:S(2)}) collective-permute-start(bf16[2,512]{1,0:T(2,128)(2,1)S(1)} %broadcast_select_fusion), channel_id=1, source_target_pairs={{0,31},{1,0},{2,1},{3,2},{4,3},{5,4},{6,5},{7,6},{8,7},{9,8},{10,9... | collective-permute-start | bytes 6152 | tf_op jit(solution)/shard_map/ppermute | solution.py:62
  18.5 43.0 %all-to-all-start = ((bf16[8,8,512]{2,1,0:T(8,128)(2,1)}), bf16[8,8,512]{2,1,0:T(8,128)(2,1)S(1)}, u32[]{:S(2)}, u32[]{:S(2)}) async-start(bf16[8,8,512]{2,1,0:T(8,128)(2,1)} %bitcast_select_fusion), calls=%async_computation | async-start | bytes 131072 | tf_op jit(solution)/shard_map/all_to_all | solution.py:46
  23.6 27.4 %collective-permute-start.1 = (bf16[4,512]{1,0:T(4,128)(2,1)S(1)}, bf16[4,512]{1,0:T(4,128)(2,1)S(1)}, u32[]{:S(2)}, u32[]{:S(2)}) collective-permute-start(bf16[4,512]{1,0:T(4,128)(2,1)S(1)} %pad_maximum_fusion.2), channel_id=1, source_target_pairs={{0,30},{1,31},{2,0},{3,1},{4,2},{5,3},{6,4},{7,5},{8,6},{9,7},{10,... | collective-permute-start | bytes 12296 | tf_op jit(solution)/shard_map/ppermute | solution.py:62
  51.0 1.0 copy-start.3
  51.0 4.6 %collective-permute-start.2 = (bf16[8,512]{1,0:T(8,128)(2,1)S(1)}, bf16[8,512]{1,0:T(8,128)(2,1)S(1)}, u32[]{:S(2)}, u32[]{:S(2)}) collective-permute-start(bf16[8,512]{1,0:T(8,128)(2,1)S(1)} %pad_maximum_fusion.1), channel_id=1, source_target_pairs={{0,28},{1,29},{2,30},{3,31},{4,0},{5,1},{6,2},{7,3},{8,4},{9,5},{1... | collective-permute-start | bytes 24584 | tf_op jit(solution)/shard_map/ppermute | solution.py:62
  52.0 3.7 %copy-start.1 = (bf16[512,512]{1,0:T(8,128)(2,1)S(1)}, bf16[512,512]{1,0:T(8,128)(2,1)}, u32[]{:S(2)}) copy-start(bf16[512,512]{1,0:T(8,128)(2,1)} %param.12) | copy-start | bytes 1572868
  53.9 4.2 %copy-start.4 = (s32[2]{0:T(128)S(1)}, s32[2]{0:T(128)}, u32[]{:S(2)}) copy-start(s32[2]{0:T(128)} %param.17) | copy-start | bytes 28
  53.9 4.3 %copy-start.2 = (s32[768]{0:T(1024)S(1)}, s32[768]{0:T(1024)}, u32[]{:S(2)}) copy-start(s32[768]{0:T(1024)} %param.15) | copy-start | bytes 9220
  55.6 1.8 collective-permute-start.3
  57.5 4.0 %collective-permute-start.4 = (bf16[32,512]{1,0:T(8,128)(2,1)S(1)}, bf16[32,512]{1,0:T(8,128)(2,1)S(1)}, u32[]{:S(2)}, u32[]{:S(2)}) collective-permute-start(bf16[32,512]{1,0:T(8,128)(2,1)S(1)} %concatenate.31), channel_id=1, source_target_pairs={{0,16},{1,17},{2,18},{3,19},{4,20},{5,21},{6,22},{7,23},{8,24},{9,... | collective-permute-start | bytes 98312 | tf_op jit(solution)/shard_map/ppermute | solution.py:62
  73.7 135.7 %all-to-all-start.1 = ((bf16[8,8,512]{2,1,0:T(8,128)(2,1)}), bf16[8,8,512]{2,1,0:T(8,128)(2,1)S(1)}, u32[]{:S(2)}, u32[]{:S(2)}) async-start(bf16[8,8,512]{2,1,0:T(8,128)(2,1)} %fusion.5), calls=%async_computation.1 | async-start | bytes 131072 | tf_op jit(solution)/shard_map/all_to_all | solution.py:91
  77.0 131.6 %all-reduce.3.cloned.1.call-start = ((), (), s32[]{:S(2)}) async-start(), calls=%async_computation.2 | async-start | bytes 262144
Sparse Core Ops, SparseCore 0:
  83.4 125.2 all-reduce.2
